TPU v7x, 256 devices: a whole 4x4x8 slice. The times are simulated.
256 devices in a mesh: chan: 128 (over x_lo, z, y, core), win: 2 (over x_hi).
Axes of the slice: x: 4 (x_hi: 2, x_lo: 2; x = x_hi * 2 + x_lo), y: 4, z: 8, core: 2. Of those that a mesh axis runs over, the one named last changes fastest.
Arguments:
- spectra: bfloat16 [8, 4096, 1024], P('win', 'chan'), may hold values from -6 to 6
- source_pool: bfloat16 [8, 32768, 1024], P('win', 'chan'), may hold values from -6 to 6
- owners: int32 [4], replicated, may hold values from 0 to 127, as said below
- source_rows: int32 [4, 128], replicated, may hold values from 0 to 255, as said below
Outputs:
- stack: bfloat16 [4096, 64, 512], P('chan', None, 'win')
Inputs may be any that keep to these rules, and one draw needn't show every extreme that they name: The owners are distinct; 0 and 127 are always among them. `source_rows`: within a block the rows are distinct; 0 and 255 are always among them.
All inputs are finite; a program needn't handle non-finite values.
Results may differ from a plain program's by a relative error of at most 0.0049.
Values may be sent and summed in bfloat16 or wider, within the bound.
A program may use at most 128 MiB of HBM per device.

v0:
```python
import jax
import jax.numpy as jnp
from jax import lax
from jax.sharding import PartitionSpec as P

LAGS = 64


def broadcast(x, axis, root):
    mine = lax.axis_index(axis) == root
    return lax.psum(jnp.where(mine, x, jnp.zeros_like(x)), axis)


def phase_tables(bins, lags):
    freq = jnp.arange(bins, dtype=jnp.float32)
    shift = (jnp.arange(lags, dtype=jnp.int32) - lags // 2).astype(jnp.float32)
    phase = jnp.pi * shift[:, None] * freq[None, :] / bins
    return (jnp.cos(phase), jnp.sin(phase))


def modulate(spec, cosine, sine, bins):
    values = spec.astype(jnp.float32)
    real_part = values[..., :bins][..., None, :]
    imag_part = values[..., bins:][..., None, :]
    scale = (2.0 * bins) ** (-0.5)
    first = (real_part * cosine - imag_part * sine) * scale
    second = (imag_part * cosine + real_part * sine) * scale
    return jnp.concatenate([first, second], axis=-1).astype(jnp.bfloat16)


def correlate(lagged, source):
    return jnp.einsum("wclk,wsk->cls", lagged, source, preferred_element_type=jnp.float32)


def flatten_blocks(blocks):
    count, windows, rows, width = blocks.shape
    return blocks.transpose(1, 0, 2, 3).reshape(windows, count * rows, width)


def on_device(spectra, source_pool, owners, source_rows):
    bins = spectra.shape[2] // 2
    cosine, sine = phase_tables(bins, LAGS)
    block_count = owners.shape[0]
    gathered = []
    for block in range(block_count):
        local_rows = jnp.take(source_pool, source_rows[block], axis=1)
        gathered.append(broadcast(local_rows, "chan", owners[block]))
    stacked = jnp.stack(gathered)
    lagged = modulate(spectra, cosine, sine, bins)
    terms = correlate(lagged, flatten_blocks(stacked))
    result = lax.psum_scatter(terms, "win", scatter_dimension=2, tiled=True)
    return result.astype(jnp.bfloat16)


def solution(mesh):
    placed = (P("win", "chan", None), P("win", "chan", None), P(), P())
    return jax.shard_map(
        on_device, mesh=mesh, in_specs=placed, out_specs=P("chan", None, "win"), check_vma=False
    )
```

profile of v0, /device:TPU:1, one launch (start us, length us, event | category | flops | bytes accessed | tf_op | source)
XLA Modules:
  0.0 1221.1 jit_solution(6014485416823943917)
XLA Ops:
  6.5 0.0 copy-start
  6.5 0.0 all-reduce.3.cloned.1.call-start
  6.5 1.5 fusion.15
  10.5 0.8 compare_and_fusion.3
  11.4 0.0 copy-done
  11.4 4.7 gather_fusion.2
  16.1 4.7 gather_fusion.3
  20.8 3.7 gather_fusion.1
  24.4 4.9 gather_fusion
  29.3 0.0 copy-start.1
  29.3 3.2 fusion.7
  32.5 2.8 fusion.9
  35.4 0.0 all-reduce.3.cloned.1.call-update
  35.4 0.0 reduce-scatter.2.cloned.1.call-start
  35.4 0.0 copy-done.1
  35.4 0.1 fusion.14
  35.5 0.2 copy.8
  35.7 0.2 copy.9
  35.9 0.5 fusion.12
  36.4 8.5 multiply_convert_fusion.1
  44.9 1090.3 %all-reduce.3.cloned.1.call-done = (bf16[1,4,128,1024]{3,2,1,0:T(8,128)(2,1)}, bf16[1,4,128,1024]{3,2,1,0:T(8,128)(2,1)}, bf16[1,4,128,1024]{3,2,1,0:T(8,128)(2,1)}, bf16[1,4,128,1024]{3,2,1,0:T(8,128)(2,1)}) async-done(((bf16[1,4,128,1024]{3,2,1,0:T(8,128)(2,1)}, bf16[1,4,128,1024]{3,2,1,0:T(8,128)(2,1)}, bf16[1,4,128,1024]{3,2,1,0:T(8,128)(2,1)}, bf16[1,4,128,1024]{3,2,1,0:T(8,128)(2,1)}), ...) | async-done | bytes 4194320 | tf_op jit(solution)/shard_map/psum | solution.py:11
  1135.2 2.4 maximum_bitcast_fusion
  1137.7 0.6 copy.10
  1138.3 13.9 %fusion.4 = f32[32,64,512]{2,1,0:T(8,128)} fusion(bf16[4,512,1024,1]{2,1,0,3:T(8,128)(2,1)S(1)} %bitcast.49, bf16[4,32,64,512]{3,2,0,1:T(8,128)(2,1)} %get-tuple-element.19, bf16[4,32,64,512]{3,2,0,1:T(8,128)(2,1)} %get-tuple-element.18), kind=kOutput, calls=%fused_computation.11 | convolution fusion | flops 8623489024 | bytes 25165824 | tf_op jit(solution)/shard_map/wclk,wsk->cls/dot_general | solution.py:32
  1152.2 0.0 reduce-scatter.2.cloned.1.call-update
  1152.2 59.4 %reduce-scatter.2.cloned.1.call-done = f32[32,64,256]{2,1,0:T(8,128)} async-done(((f32[32,64,512]{2,1,0:T(8,128)}), f32[32,64,256]{2,1,0:T(8,128)}) %reduce-scatter.2.cloned.1.call-update) | async-done | bytes 2097168 | tf_op jit(solution)/shard_map/reduce_scatter | solution.py:51
  1211.6 2.7 convert_element_type.22
  (5 shorter events, 0.0 us)
Async XLA Ops:
  6.5 4.9 copy-start
  6.5 1128.7 %all-reduce.3.cloned.1.call-start = ((), (), s32[]{:S(2)}) async-start(), calls=%async_computation.2 | async-start | bytes 8388608 | tf_op jit(solution)/shard_map/psum | solution.py:11
  29.3 6.1 copy-start.1
  35.4 1176.2 %reduce-scatter.2.cloned.1.call-start = ((), (), s32[]{:S(2)}) async-start(), calls=%async_computation.1 | async-start | bytes 6291456 | tf_op jit(solution)/shard_map/reduce_scatter | solution.py:51
Sparse Core Ops, SparseCore 0:
  35.5 1099.6 all-reduce.2
  1152.3 59.2 reduce-scatter.1
where the time goes:
time: 1220 us
  waiting for transfers between devices  1150 us (94%)
  other arithmetic  21.1 us (2%)
  local copies, waits for them, and re-layouts  20.4 us (2%)
  between operations  16 us (1%)
  matrix products  13.9 us (1%)
    psum x1, waiting for transfers between devices, broadcast(): return lax.psum(jnp.where(mine, x, jnp.zeros_like(x)), axis)  1090 us
    reduce_scatter x1, waiting for transfers between devices, on_device(): result = lax.psum_scatter(terms, 'win', scatter_dimension=2, tiled=True)  59.4 us
  transfers between devices with their start and end apart: 2, of which 2 were waited for; matrix products, arithmetic and copies ran while one was open for 1% of the time, Pallas kernels for 0%

commit v1 on v0

v1 whole, which is shorter than its diff:
```python
import functools

import jax
import jax.numpy as jnp
import numpy as np
from jax import lax
from jax.experimental import pallas as pl
from jax.experimental.pallas import tpu as pltpu
from jax.sharding import PartitionSpec as P

LAGS = 64
BINS = 512
LANES = 128
MESH = pl.DeviceIdType.MESH
NX, NZ, NY, NC, NH = 2, 8, 4, 2, 2
PLANE = NX * NY * NC
COLUMN = NH * NZ
WAVES = 2


def phase_tables():
    freq = np.arange(BINS, dtype=np.float64)
    shift = np.arange(LAGS, dtype=np.float64) - LAGS // 2
    phase = np.pi * shift[:, None] * freq[None, :] / BINS
    scale = (2.0 * BINS) ** -0.5
    return (
        (np.cos(phase) * scale).astype(np.float32),
        (np.sin(phase) * scale).astype(np.float32),
    )


def kernel(
    owners, rows_ref, cos_ref, sin_ref, spec_ref, pool_hbm, out_ref,
    pool, mine, cand_a, cand_b, slots, cand2_a, cand2_b, red, pieces, spec_in, spec32, mod, acc,
    pool_sem, rs1_send, rs1_recv, rs2_send, rs2_recv, ag1_send, ag1_recv,
    ring_send, ring_recv, sib_send, sib_recv, spec_send, spec_recv,
):
    chan = lax.axis_index("chan")
    half = lax.axis_index("win")
    x, z = chan // 64, (chan // 8) % 8
    y, core = (chan // 2) % 4, chan % 2
    q = x * NY + y
    s = q * NC + core
    t = half * NZ + z

    def device(x, y, z, core, half):
        return (x * 64 + z * 8 + y * 2 + core, half)

    def plane_device(index):
        return device(index // 8, (index // 2) % 4, z, index % 2, half)

    def column_device(index):
        return device(x, y, index % NZ, core, index // NZ)

    def piece(v, zz, cc):
        return (v * NZ + zz) * NC + cc

    up = device(x, y, (z + 1) % NZ, core, half)
    down = device(x, y, (z + NZ - 1) % NZ, core, half)
    sibling = device(x, y, z, 1 - core, half)
    partner = device(x, y, z, core, 1 - half)

    loads = []
    for w in range(4):
        load = pltpu.make_async_copy(pool_hbm.at[w], pool.at[w], pool_sem.at[w])
        load.start()
        loads.append(load)

    barrier = pltpu.get_barrier_semaphore()
    for j in range(1, PLANE):
        pl.semaphore_signal(
            barrier, inc=1, device_id=plane_device((s + j) % PLANE), device_id_type=MESH
        )
    for j in range(1, COLUMN):
        pl.semaphore_signal(
            barrier, inc=1, device_id=column_device((t + j) % COLUMN), device_id_type=MESH
        )

    target = jnp.full((128, 1), -1, jnp.int32)
    for b in range(4):
        target = jnp.where(owners[b] == chan, rows_ref[:, b : b + 1], target)
    onehot = (lax.broadcasted_iota(jnp.int32, (128, 256), 1) == target).astype(jnp.float32)
    onehot = onehot.astype(jnp.bfloat16)
    for w in range(4):
        loads[w].wait()
        picked = jnp.dot(onehot, pool[w], preferred_element_type=jnp.float32)
        picked = picked.astype(jnp.bfloat16)
        for group in range(8):
            kh, cc, v = group // 4, (group // 2) % 2, group % 2
            for qq in range(8):
                mine[v, qq * NC + cc, 2 * w + kh] = picked[
                    qq * 16 : qq * 16 + 16, group * LANES : (group + 1) * LANES
                ]

    pl.semaphore_wait(barrier, PLANE + COLUMN - 2)

    sends = []
    cand, cand2 = (cand_a, cand_b), (cand2_a, cand2_b)

    def remote(src, dst, send_sem, recv_sem, where):
        copy = pltpu.make_async_remote_copy(
            src_ref=src, dst_ref=dst, send_sem=send_sem, recv_sem=recv_sem,
            device_id=where, device_id_type=MESH,
        )
        return copy

    def send(*args):
        copy = remote(*args)
        copy.start()
        sends.append(copy)

    def wait_recv(ref, recv_sem):
        remote(ref, ref, recv_sem, recv_sem, sibling).wait_recv()

    for v in range(WAVES):
        for j in range(1, PLANE):
            to = (s + j) % PLANE
            send(mine.at[v, to], cand[v].at[s], rs1_send.at[v, j], rs1_recv.at[v, s], plane_device(to))
        cand[v][s] = mine[v, s]
    send(spec_ref, spec_in, spec_send, spec_recv, partner)

    def modulate(hh):
        def body(i, carry):
            w, r = i // 8, (i % 8) * 4
            for g in range(4):
                cosine = cos_ref[:, g * LANES : (g + 1) * LANES]
                sine = sin_ref[:, g * LANES : (g + 1) * LANES]
                for k in range(4):
                    row = pl.ds(r + k, 8, stride=0)
                    a = jnp.tile(spec32[w, g, row, :], (8, 1))
                    b = jnp.tile(spec32[w, 4 + g, row, :], (8, 1))
                    first = (a * cosine - b * sine).astype(jnp.bfloat16)
                    second = (b * cosine + a * sine).astype(jnp.bfloat16)
                    at = pl.ds(pl.multiple_of((r + k) * LAGS, LAGS), LAGS)
                    mod[piece(g % 2, 2 * w, g // 2), hh, at, :] = first
                    mod[piece(g % 2, 2 * w + 1, g // 2), hh, at, :] = second
            return carry

        lax.fori_loop(0, 32, body, 0)

    def widen(ref):
        for g in range(8):
            spec32[:, g] = ref[:, :, g * LANES : (g + 1) * LANES].astype(jnp.float32)

    widen(spec_ref)
    modulate(half)

    for v in range(WAVES):
        for j in range(1, PLANE):
            frm = (s + j) % PLANE
            wait_recv(cand[v].at[frm], rs1_recv.at[v, frm])
        for b in range(4):
            at = (owners[b] // 64) * 8 + owners[b] % 8
            slots[v, b // 2, :, b % 2] = cand[v][at]
        for j in range(1, COLUMN):
            to = (t + j) % COLUMN
            send(slots.at[v, to // NZ, to % NZ], cand2[v].at[half, z], rs2_send.at[v, j], rs2_recv.at[v, t], column_device(to))
        cand2[v][half, z] = slots[v, half, z]

    wait_recv(spec_in, spec_recv)
    widen(spec_in)
    modulate(1 - half)

    for v in range(WAVES):
        for j in range(1, COLUMN):
            frm = (t + j) % COLUMN
            wait_recv(cand2[v].at[frm // NZ, frm % NZ], rs2_recv.at[v, frm])
        for hh in range(NH):
            for bb in range(2):
                zz = (owners[2 * half + bb] // 8) % 8
                red[v, 2 * hh + bb] = cand2[v][hh, zz, bb]
        for j in range(1, NX * NY):
            to = (q + j) % (NX * NY)
            p = piece(v, z, core)
            send(red.at[v], pieces.at[p, :, q], ag1_send.at[v, j], ag1_recv.at[v, q], device(to // 4, to % 4, z, core, half))
        pieces[piece(v, z, core), :, q] = red[v]

    def multiply(indices, start):
        total = len(indices)

        def body(i, carry):
            at = pl.ds(pl.multiple_of(i * 1024, 1024), 1024)
            result = None
            for p in indices:
                left = jnp.concatenate([mod[p, 0, at, :], mod[p, 1, at, :]], axis=1)
                right = jnp.concatenate(
                    [pieces[p, 0:2].reshape(256, LANES), pieces[p, 2:4].reshape(256, LANES)], axis=1
                )
                term = lax.dot_general(
                    left, right, (((1,), (1,)), ((), ())), preferred_element_type=jnp.float32
                )
                result = term if result is None else result + term
            if not start:
                result = result + acc[at, :]
            acc[at, :] = result
            return carry

        lax.fori_loop(0, 2, body, 0)

    def forward(v, zz):
        p = piece(v, zz, core)
        send(pieces.at[p], pieces.at[p], sib_send.at[v, zz], sib_recv.at[v, zz], sibling)

    for v in range(WAVES):
        p = piece(v, z, core)
        for j in range(1, NX * NY):
            frm = (q + j) % (NX * NY)
            wait_recv(pieces.at[p, :, frm], ag1_recv.at[v, frm])
        send(pieces.at[p], pieces.at[p], ring_send.at[v, 0, 0], ring_recv.at[v, 0, 0], up)
        send(pieces.at[p], pieces.at[p], ring_send.at[v, 0, 1], ring_recv.at[v, 0, 1], down)
        forward(v, z)

    multiply([piece(0, z, core), piece(1, z, core)], True)

    def sibling_ready(v, zz):
        p = piece(v, zz, 1 - core)
        wait_recv(pieces.at[p], sib_recv.at[v, zz])

    ready = [z]
    for d in range(1, 5):
        below, above = (z + NZ - d) % NZ, (z + d) % NZ
        for v in range(WAVES):
            pb, pa = piece(v, below, core), piece(v, above, core)
            if d < 4:
                wait_recv(pieces.at[pb], ring_recv.at[v, d - 1, 0])
                if d < 3:
                    send(pieces.at[pb], pieces.at[pb], ring_send.at[v, d, 0], ring_recv.at[v, d, 0], up)
                else:
                    part = pieces.at[pb, 0:2]
                    send(part, part, ring_send.at[v, d, 0], ring_recv.at[v, d, 0], up)
                forward(v, below)
                wait_recv(pieces.at[pa], ring_recv.at[v, d - 1, 1])
                if d < 3:
                    send(pieces.at[pa], pieces.at[pa], ring_send.at[v, d, 1], ring_recv.at[v, d, 1], down)
                else:
                    part = pieces.at[pa, 2:4]
                    send(part, part, ring_send.at[v, d, 1], ring_recv.at[v, d, 1], down)
                forward(v, above)
            else:
                wait_recv(pieces.at[pb, 0:2], ring_recv.at[v, d - 1, 0])
                wait_recv(pieces.at[pa, 2:4], ring_recv.at[v, d - 1, 1])
                forward(v, below)
        for zz in ready:
            for v in range(WAVES):
                sibling_ready(v, zz)
            multiply([piece(0, zz, 1 - core), piece(1, zz, 1 - core)], False)
        ready = [below, above] if d < 4 else [below]
        for zz in ready:
            multiply([piece(0, zz, core), piece(1, zz, core)], False)
    for zz in ready:
        for v in range(WAVES):
            sibling_ready(v, zz)
        multiply([piece(0, zz, 1 - core), piece(1, zz, 1 - core)], False)

    out_ref[...] = acc[...].astype(jnp.bfloat16)
    for copy in sends:
        copy.wait_send()


def on_device(spectra, source_pool, owners, source_rows):
    cosine, sine = phase_tables()
    vmem = pl.BlockSpec(memory_space=pltpu.VMEM)
    dma = pltpu.SemaphoreType.DMA
    b16 = jnp.bfloat16
    out = pl.pallas_call(
        kernel,
        out_shape=jax.ShapeDtypeStruct((32 * LAGS, 256), b16),
        in_specs=[pl.BlockSpec(memory_space=pltpu.SMEM), vmem, vmem, vmem, vmem, pl.BlockSpec(memory_space=pl.ANY)],
        out_specs=vmem,
        scratch_shapes=[
            pltpu.VMEM((4, 256, 1024), b16),
            pltpu.VMEM((WAVES, PLANE, 8, 16, LANES), b16),
            pltpu.VMEM((PLANE, 8, 16, LANES), b16),
            pltpu.VMEM((PLANE, 8, 16, LANES), b16),
            pltpu.VMEM((WAVES, NH, NZ, 2, 16, LANES), b16),
            pltpu.VMEM((NH, NZ, 2, 16, LANES), b16),
            pltpu.VMEM((NH, NZ, 2, 16, LANES), b16),
            pltpu.VMEM((WAVES, 4, 16, LANES), b16),
            pltpu.VMEM((WAVES * NZ * NC, 4, 8, 16, LANES), b16),
            pltpu.VMEM((4, 32, 1024), b16),
            pltpu.VMEM((4, 8, 32, LANES), jnp.float32),
            pltpu.VMEM((WAVES * NZ * NC, NH, 32 * LAGS, LANES), b16),
            pltpu.VMEM((32 * LAGS, 256), jnp.float32),
            dma((4,)),
            dma((WAVES, PLANE)),
            dma((WAVES, PLANE)),
            dma((WAVES, COLUMN)),
            dma((WAVES, COLUMN)),
            dma((WAVES, 8)),
            dma((WAVES, 8)),
            dma((WAVES, 4, 2)),
            dma((WAVES, 4, 2)),
            dma((WAVES, NZ)),
            dma((WAVES, NZ)),
            dma,
            dma,
        ],
        compiler_params=pltpu.CompilerParams(
            collective_id=0, has_side_effects=True, vmem_limit_bytes=62 * 2**20
        ),
    )(owners, source_rows.T, jnp.asarray(cosine), jnp.asarray(sine), spectra, source_pool)
    return out.reshape(32, LAGS, 256)


def solution(mesh):
    placed = (P("win", "chan", None), P("win", "chan", None), P(), P())
    return jax.shard_map(
        on_device, mesh=mesh, in_specs=placed, out_specs=P("chan", None, "win"), check_vma=False
    )
```

time: 1220 us -> 75.6 us (0.06)
  waiting for transfers between devices: 1150 us -> 0 us
  Pallas kernels: 0 us -> 71.6 us
  other arithmetic: 21.1 us -> 0 us
  local copies, waits for them, and re-layouts: 20.4 us -> 3.72 us
  between operations: 16 us -> 0.01 us
  matrix products: 13.9 us -> 0 us
    psum x1 -> x0, waiting for transfers between devices: 1090 us -> none  [broadcast(): return lax.psum(jnp.where(mine, x, jnp.zeros_like(x)), axis)]
    pallas_call x0 -> x1, Pallas kernels: none -> 71.6 us  [on_device(): pl.pallas_call(kernel, out_shape=jax.ShapeDtypeStruct((32 * LAGS, 256), b...]
    reduce_scatter x1 -> x0, waiting for transfers between devices: 59.4 us -> none  [on_device(): result = lax.psum_scatter(terms, 'win', scatter_dimension=2, tiled=True)]
    gather x4 -> x0, local copies, waits for them, and re-layouts: 17.9 us -> none  [on_device(): local_rows = jnp.take(source_pool, source_rows[block], axis=1)]
    another operation x3 -> x0, other arithmetic: 14.5 us -> none
    dot_general x1 -> x0, matrix products: 13.9 us -> none  [correlate(): jnp.einsum('wclk,wsk->cls', lagged, source, preferred_element_type=jnp.fl...]
  transfers between devices with their start and end apart: 2 -> 0, of which waited for: 2 -> 0; matrix products, arithmetic and copies ran while one was open for 1% -> 0% of each run, Pallas kernels for 0% -> 0%
where the time goes in v1:
time: 75.6 us; the launch traced here: 75.3 us
  Pallas kernels  71.6 us (95%)
  local copies, waits for them, and re-layouts  3.72 us (5%)
    pallas_call x1, Pallas kernels, on_device(): pl.pallas_call(kernel, out_shape=jax.ShapeDtypeStruct((32 * LAGS, 256), b...  71.6 us
    unnamed x2, local copies, waits for them, and re-layouts  3.72 us

profile of v1, /device:TPU:1, one launch (start us, length us, event | category | flops | bytes accessed | tf_op | source)
XLA Modules:
  0.0 75.3 jit_solution(10598955096330616001)
XLA Ops:
  0.0 1.4 %copy.7 = s32[4,128]{0,1:T(8,128)} copy(s32[4,128]{1,0:T(4,128)} %param.9) | data formatting | bytes 4096 | tf_op args[3]
  1.4 71.6 %shard_map.64 = bf16[2048,256]{1,0:T(8,128)(2,1)} custom-call(s32[4]{0:T(128)} %owners.1, s32[128,4]{1,0:T(8,128)} %bitcast.3, f32[64,512]{1,0:T(8,128)} %constant.4.clone.cos_ref, f32[64,512]{1,0:T(8,128)} %constant.5.clone.sin_ref, bf16[4,32,1024]{2,1,0:T(8,128)(2,1)} %spec_ref.1, bf16[4,256,1024]{2,1,0:T(8,128)(2,1)} %pool_hbm.1), custom_call_target="tpu_custom_call" | custom-call | tf_op jit(solution)/shard_map/pallas_call | solution.py:265
  73.0 2.3 %copy.9 = bf16[32,64,256]{2,1,0:T(8,128)(2,1)} copy(bf16[32,64,256]{2,1,0:T(8,128)(2,1)} %bitcast.2) | data formatting | bytes 2097152

commit v2 on v1

--- a/solution.py
+++ b/solution.py
@@ -16,6 +16,7 @@
 PLANE = NX * NY * NC
 COLUMN = NH * NZ
 WAVES = 2
+ROWS = 512
 
 
 def phase_tables():
@@ -119,7 +120,7 @@
         cand[v][s] = mine[v, s]
     send(spec_ref, spec_in, spec_send, spec_recv, partner)
 
-    def modulate(hh):
+    def modulate(hh, first_window, last_window):
         def body(i, carry):
             w, r = i // 8, (i % 8) * 4
             for g in range(4):
@@ -136,14 +137,14 @@
                     mod[piece(g % 2, 2 * w + 1, g // 2), hh, at, :] = second
             return carry
 
-        lax.fori_loop(0, 32, body, 0)
+        lax.fori_loop(8 * first_window, 8 * last_window, body, 0)
 
     def widen(ref):
         for g in range(8):
             spec32[:, g] = ref[:, :, g * LANES : (g + 1) * LANES].astype(jnp.float32)
 
     widen(spec_ref)
-    modulate(half)
+    modulate(half, 0, 4)
 
     for v in range(WAVES):
         for j in range(1, PLANE):
@@ -159,7 +160,7 @@
 
     wait_recv(spec_in, spec_recv)
     widen(spec_in)
-    modulate(1 - half)
+    modulate(1 - half, 0, 2)
 
     for v in range(WAVES):
         for j in range(1, COLUMN):
@@ -175,27 +176,29 @@
             send(red.at[v], pieces.at[p, :, q], ag1_send.at[v, j], ag1_recv.at[v, q], device(to // 4, to % 4, z, core, half))
         pieces[piece(v, z, core), :, q] = red[v]
 
+    modulate(1 - half, 2, 3)
+
     def multiply(indices, start):
-        total = len(indices)
-
         def body(i, carry):
-            at = pl.ds(pl.multiple_of(i * 1024, 1024), 1024)
-            result = None
-            for p in indices:
-                left = jnp.concatenate([mod[p, 0, at, :], mod[p, 1, at, :]], axis=1)
-                right = jnp.concatenate(
-                    [pieces[p, 0:2].reshape(256, LANES), pieces[p, 2:4].reshape(256, LANES)], axis=1
-                )
-                term = lax.dot_general(
-                    left, right, (((1,), (1,)), ((), ())), preferred_element_type=jnp.float32
-                )
-                result = term if result is None else result + term
+            at = pl.ds(pl.multiple_of(i * ROWS, ROWS), ROWS)
+            left = jnp.concatenate([mod[p, hh, at, :] for p in indices for hh in range(NH)], axis=1)
+            right = jnp.concatenate(
+                [
+                    pieces[p, 2 * hh : 2 * hh + 2].reshape(256, LANES)
+                    for p in indices
+                    for hh in range(NH)
+                ],
+                axis=1,
+            )
+            result = lax.dot_general(
+                left, right, (((1,), (1,)), ((), ())), preferred_element_type=jnp.float32
+            )
             if not start:
                 result = result + acc[at, :]
             acc[at, :] = result
             return carry
 
-        lax.fori_loop(0, 2, body, 0)
+        lax.fori_loop(0, 32 * LAGS // ROWS, body, 0)
 
     def forward(v, zz):
         p = piece(v, zz, core)
@@ -210,6 +213,7 @@
         send(pieces.at[p], pieces.at[p], ring_send.at[v, 0, 1], ring_recv.at[v, 0, 1], down)
         forward(v, z)
 
+    modulate(1 - half, 3, 4)
     multiply([piece(0, z, core), piece(1, z, core)], True)
 
     def sibling_ready(v, zz):
@@ -243,10 +247,10 @@
         for zz in ready:
             for v in range(WAVES):
                 sibling_ready(v, zz)
-            multiply([piece(0, zz, 1 - core), piece(1, zz, 1 - core)], False)
+        indices = [piece(v, zz, 1 - core) for zz in ready for v in range(WAVES)]
         ready = [below, above] if d < 4 else [below]
-        for zz in ready:
-            multiply([piece(0, zz, core), piece(1, zz, core)], False)
+        indices += [piece(v, zz, core) for zz in ready for v in range(WAVES)]
+        multiply(indices, False)
     for zz in ready:
         for v in range(WAVES):
             sibling_ready(v, zz)

time: 75.6 us -> 72.6 us (0.960)
  Pallas kernels: 71.6 us -> 68.7 us
    pallas_call x1, Pallas kernels: 71.6 us -> 68.7 us  [on_device(): pl.pallas_call(kernel, out_shape=jax.ShapeDtypeStruct((32 * LAGS, 256), b...]
where the time goes in v2:
time: 72.6 us; the launch traced here: 72.5 us
  Pallas kernels  68.7 us (95%)
  local copies, waits for them, and re-layouts  3.72 us (5%)
    pallas_call x1, Pallas kernels, on_device(): pl.pallas_call(kernel, out_shape=jax.ShapeDtypeStruct((32 * LAGS, 256), b...  68.7 us
    unnamed x2, local copies, waits for them, and re-layouts  3.72 us

profile of v2, /device:TPU:1, one launch (start us, length us, event | category | flops | bytes accessed | tf_op | source)
XLA Modules:
  0.0 72.5 jit_solution(7912215871206255708)
XLA Ops:
  0.0 1.4 %copy.7 = s32[4,128]{0,1:T(8,128)} copy(s32[4,128]{1,0:T(4,128)} %param.9) | data formatting | bytes 4096 | tf_op args[3]
  1.4 68.7 %shard_map.64 = bf16[2048,256]{1,0:T(8,128)(2,1)} custom-call(s32[4]{0:T(128)} %owners.1, s32[128,4]{1,0:T(8,128)} %bitcast.3, f32[64,512]{1,0:T(8,128)} %constant.4.clone.cos_ref, f32[64,512]{1,0:T(8,128)} %constant.5.clone.sin_ref, bf16[4,32,1024]{2,1,0:T(8,128)(2,1)} %spec_ref.1, bf16[4,256,1024]{2,1,0:T(8,128)(2,1)} %pool_hbm.1), custom_call_target="tpu_custom_call" | custom-call | tf_op jit(solution)/shard_map/pallas_call | solution.py:269
  70.2 2.3 %copy.9 = bf16[32,64,256]{2,1,0:T(8,128)(2,1)} copy(bf16[32,64,256]{2,1,0:T(8,128)(2,1)} %bitcast.2) | data formatting | bytes 2097152

commit v3 on v2

--- a/solution.py
+++ b/solution.py
@@ -34,6 +34,7 @@
     owners, rows_ref, cos_ref, sin_ref, spec_ref, pool_hbm, out_ref,
     pool, mine, cand_a, cand_b, slots, cand2_a, cand2_b, red, pieces, spec_in, spec32, mod, acc,
     pool_sem, rs1_send, rs1_recv, rs2_send, rs2_recv, ag1_send, ag1_recv,
+    agz_send, agz_recv, agxy_send, agxy_recv,
     ring_send, ring_recv, sib_send, sib_recv, spec_send, spec_recv,
 ):
     chan = lax.axis_index("chan")
@@ -170,13 +171,19 @@
             for bb in range(2):
                 zz = (owners[2 * half + bb] // 8) % 8
                 red[v, 2 * hh + bb] = cand2[v][hh, zz, bb]
+        p = piece(v, z, core)
+        slot = pieces.at[p, :, q]
+        if v == 1:
+            for j in range(1, NZ):
+                send(red.at[1], slot, agz_send.at[j], agz_recv.at[z], device(x, y, (z + j) % NZ, core, half))
         for j in range(1, NX * NY):
             to = (q + j) % (NX * NY)
-            p = piece(v, z, core)
-            send(red.at[v], pieces.at[p, :, q], ag1_send.at[v, j], ag1_recv.at[v, q], device(to // 4, to % 4, z, core, half))
-        pieces[piece(v, z, core), :, q] = red[v]
-
-    modulate(1 - half, 2, 3)
+            where = device(to // 4, to % 4, z, core, half)
+            if v == 0:
+                send(red.at[0], slot, ag1_send.at[j], ag1_recv.at[q], where)
+            else:
+                send(red.at[1], slot, agxy_send.at[z, j], agxy_recv.at[z, q], where)
+        pieces[p, :, q] = red[v]
 
     def multiply(indices, start):
         def body(i, carry):
@@ -204,15 +211,29 @@
         p = piece(v, zz, core)
         send(pieces.at[p], pieces.at[p], sib_send.at[v, zz], sib_recv.at[v, zz], sibling)
 
-    for v in range(WAVES):
-        p = piece(v, z, core)
+    p = piece(0, z, core)
+    for j in range(1, NX * NY):
+        frm = (q + j) % (NX * NY)
+        wait_recv(pieces.at[p, :, frm], ag1_recv.at[frm])
+    send(pieces.at[p], pieces.at[p], ring_send.at[0, 0], ring_recv.at[0, 0], up)
+    send(pieces.at[p], pieces.at[p], ring_send.at[0, 1], ring_recv.at[0, 1], down)
+    forward(0, z)
+    for d in (1, 7, 2, 6, 3, 5, 4):
+        zz = (z + d) % NZ
+        slot = pieces.at[piece(1, zz, core), :, q]
+        wait_recv(slot, agz_recv.at[zz])
+        for j in range(1, NX * NY):
+            to = (q + j) % (NX * NY)
+            send(slot, slot, agxy_send.at[zz, j], agxy_recv.at[zz, q], device(to // 4, to % 4, z, core, half))
+
+    def plane_ready(zz):
         for j in range(1, NX * NY):
             frm = (q + j) % (NX * NY)
-            wait_recv(pieces.at[p, :, frm], ag1_recv.at[v, frm])
-        send(pieces.at[p], pieces.at[p], ring_send.at[v, 0, 0], ring_recv.at[v, 0, 0], up)
-        send(pieces.at[p], pieces.at[p], ring_send.at[v, 0, 1], ring_recv.at[v, 0, 1], down)
-        forward(v, z)
-
+            wait_recv(pieces.at[piece(1, zz, core), :, frm], agxy_recv.at[zz, frm])
+        forward(1, zz)
+
+    modulate(1 - half, 2, 3)
+    plane_ready(z)
     modulate(1 - half, 3, 4)
     multiply([piece(0, z, core), piece(1, z, core)], True)
 
@@ -223,27 +244,28 @@
     ready = [z]
     for d in range(1, 5):
         below, above = (z + NZ - d) % NZ, (z + d) % NZ
-        for v in range(WAVES):
-            pb, pa = piece(v, below, core), piece(v, above, core)
-            if d < 4:
-                wait_recv(pieces.at[pb], ring_recv.at[v, d - 1, 0])
-                if d < 3:
-                    send(pieces.at[pb], pieces.at[pb], ring_send.at[v, d, 0], ring_recv.at[v, d, 0], up)
-                else:
-                    part = pieces.at[pb, 0:2]
-                    send(part, part, ring_send.at[v, d, 0], ring_recv.at[v, d, 0], up)
-                forward(v, below)
-                wait_recv(pieces.at[pa], ring_recv.at[v, d - 1, 1])
-                if d < 3:
-                    send(pieces.at[pa], pieces.at[pa], ring_send.at[v, d, 1], ring_recv.at[v, d, 1], down)
-                else:
-                    part = pieces.at[pa, 2:4]
-                    send(part, part, ring_send.at[v, d, 1], ring_recv.at[v, d, 1], down)
-                forward(v, above)
+        pb, pa = piece(0, below, core), piece(0, above, core)
+        if d < 4:
+            wait_recv(pieces.at[pb], ring_recv.at[d - 1, 0])
+            if d < 3:
+                send(pieces.at[pb], pieces.at[pb], ring_send.at[d, 0], ring_recv.at[d, 0], up)
             else:
-                wait_recv(pieces.at[pb, 0:2], ring_recv.at[v, d - 1, 0])
-                wait_recv(pieces.at[pa, 2:4], ring_recv.at[v, d - 1, 1])
-                forward(v, below)
+                part = pieces.at[pb, 0:2]
+                send(part, part, ring_send.at[d, 0], ring_recv.at[d, 0], up)
+            forward(0, below)
+            wait_recv(pieces.at[pa], ring_recv.at[d - 1, 1])
+            if d < 3:
+                send(pieces.at[pa], pieces.at[pa], ring_send.at[d, 1], ring_recv.at[d, 1], down)
+            else:
+                part = pieces.at[pa, 2:4]
+                send(part, part, ring_send.at[d, 1], ring_recv.at[d, 1], down)
+            forward(0, above)
+        else:
+            wait_recv(pieces.at[pb, 0:2], ring_recv.at[d - 1, 0])
+            wait_recv(pieces.at[pa, 2:4], ring_recv.at[d - 1, 1])
+            forward(0, below)
+        for zz in (below, above)[: 2 if d < 4 else 1]:
+            plane_ready(zz)
         for zz in ready:
             for v in range(WAVES):
                 sibling_ready(v, zz)
@@ -290,10 +312,14 @@
             dma((WAVES, PLANE)),
             dma((WAVES, COLUMN)),
             dma((WAVES, COLUMN)),
-            dma((WAVES, 8)),
-            dma((WAVES, 8)),
-            dma((WAVES, 4, 2)),
-            dma((WAVES, 4, 2)),
+            dma((8,)),
+            dma((8,)),
+            dma((NZ,)),
+            dma((NZ,)),
+            dma((NZ, 8)),
+            dma((NZ, 8)),
+            dma((4, 2)),
+            dma((4, 2)),
             dma((WAVES, NZ)),
             dma((WAVES, NZ)),
             dma,

time: 72.6 us -> 69.9 us (0.963)
  Pallas kernels: 68.7 us -> 66 us
    pallas_call x1, Pallas kernels: 68.7 us -> 66 us  [on_device(): pl.pallas_call(kernel, out_shape=jax.ShapeDtypeStruct((32 * LAGS, 256), b...]
where the time goes in v3:
time: 69.9 us; the launch traced here: 69.8 us
  Pallas kernels  66 us (94%)
  local copies, waits for them, and re-layouts  3.72 us (5%)
    pallas_call x1, Pallas kernels, on_device(): pl.pallas_call(kernel, out_shape=jax.ShapeDtypeStruct((32 * LAGS, 256), b...  66 us
    unnamed x2, local copies, waits for them, and re-layouts  3.72 us

profile of v3, /device:TPU:1, one launch (start us, length us, event | category | flops | bytes accessed | tf_op | source)
XLA Modules:
  0.0 69.8 jit_solution(13982333953337031913)
XLA Ops:
  0.0 1.4 %copy.7 = s32[4,128]{0,1:T(8,128)} copy(s32[4,128]{1,0:T(4,128)} %param.9) | data formatting | bytes 4096 | tf_op args[3]
  1.4 66.0 %shard_map.64 = bf16[2048,256]{1,0:T(8,128)(2,1)} custom-call(s32[4]{0:T(128)} %owners.1, s32[128,4]{1,0:T(8,128)} %bitcast.3, f32[64,512]{1,0:T(8,128)} %constant.4.clone.cos_ref, f32[64,512]{1,0:T(8,128)} %constant.5.clone.sin_ref, bf16[4,32,1024]{2,1,0:T(8,128)(2,1)} %spec_ref.1, bf16[4,256,1024]{2,1,0:T(8,128)(2,1)} %pool_hbm.1), custom_call_target="tpu_custom_call" | custom-call | tf_op jit(solution)/shard_map/pallas_call | solution.py:291
  67.5 2.3 %copy.9 = bf16[32,64,256]{2,1,0:T(8,128)(2,1)} copy(bf16[32,64,256]{2,1,0:T(8,128)(2,1)} %bitcast.2) | data formatting | bytes 2097152

commit v4 on v3

--- a/solution.py
+++ b/solution.py
@@ -185,7 +185,7 @@
                 send(red.at[1], slot, agxy_send.at[z, j], agxy_recv.at[z, q], where)
         pieces[p, :, q] = red[v]
 
-    def multiply(indices, start):
+    def multiply(indices, start, last=False):
         def body(i, carry):
             at = pl.ds(pl.multiple_of(i * ROWS, ROWS), ROWS)
             left = jnp.concatenate([mod[p, hh, at, :] for p in indices for hh in range(NH)], axis=1)
@@ -202,7 +202,10 @@
             )
             if not start:
                 result = result + acc[at, :]
-            acc[at, :] = result
+            if last:
+                out_ref[at, :] = result.astype(jnp.bfloat16)
+            else:
+                acc[at, :] = result
             return carry
 
         lax.fori_loop(0, 32 * LAGS // ROWS, body, 0)
@@ -240,6 +243,12 @@
     def sibling_ready(v, zz):
         p = piece(v, zz, 1 - core)
         wait_recv(pieces.at[p], sib_recv.at[v, zz])
+
+    def products(ready, cc, last):
+        for zz in ready:
+            for v in range(WAVES):
+                sibling_ready(v, zz)
+        multiply([piece(v, zz, cc) for zz in ready for v in range(WAVES)], False, last)
 
     ready = [z]
     for d in range(1, 5):
@@ -261,24 +270,25 @@
                 send(part, part, ring_send.at[d, 1], ring_recv.at[d, 1], down)
             forward(0, above)
         else:
+            products(ready, 1 - core, False)
             wait_recv(pieces.at[pb, 0:2], ring_recv.at[d - 1, 0])
             wait_recv(pieces.at[pa, 2:4], ring_recv.at[d - 1, 1])
             forward(0, below)
         for zz in (below, above)[: 2 if d < 4 else 1]:
             plane_ready(zz)
-        for zz in ready:
-            for v in range(WAVES):
-                sibling_ready(v, zz)
-        indices = [piece(v, zz, 1 - core) for zz in ready for v in range(WAVES)]
-        ready = [below, above] if d < 4 else [below]
-        indices += [piece(v, zz, core) for zz in ready for v in range(WAVES)]
-        multiply(indices, False)
-    for zz in ready:
-        for v in range(WAVES):
-            sibling_ready(v, zz)
-        multiply([piece(0, zz, 1 - core), piece(1, zz, 1 - core)], False)
-
-    out_ref[...] = acc[...].astype(jnp.bfloat16)
+        if d < 4:
+            for zz in ready:
+                for v in range(WAVES):
+                    sibling_ready(v, zz)
+            indices = [piece(v, zz, 1 - core) for zz in ready for v in range(WAVES)]
+            ready = [below, above]
+            indices += [piece(v, zz, core) for zz in ready for v in range(WAVES)]
+            multiply(indices, False)
+        else:
+            ready = [below]
+            multiply([piece(v, below, core) for v in range(WAVES)], False)
+    products(ready, 1 - core, True)
+
     for copy in sends:
         copy.wait_send()
 

time: 69.9 us -> 71.7 us (1.026)
  Pallas kernels: 66 us -> 67.8 us
    pallas_call x1, Pallas kernels: 66 us -> 67.8 us  [on_device(): pl.pallas_call(kernel, out_shape=jax.ShapeDtypeStruct((32 * LAGS, 256), b...]
where the time goes in v4:
time: 71.7 us; the launch traced here: 71.6 us
  Pallas kernels  67.8 us (95%)
  local copies, waits for them, and re-layouts  3.72 us (5%)
    pallas_call x1, Pallas kernels, on_device(): pl.pallas_call(kernel, out_shape=jax.ShapeDtypeStruct((32 * LAGS, 256), b...  67.8 us
    unnamed x2, local copies, waits for them, and re-layouts  3.72 us

profile of v4, /device:TPU:1, one launch (start us, length us, event | category | flops | bytes accessed | tf_op | source)
XLA Modules:
  0.0 71.6 jit_solution(9797344892390721397)
XLA Ops:
  0.0 1.4 %copy.7 = s32[4,128]{0,1:T(8,128)} copy(s32[4,128]{1,0:T(4,128)} %param.9) | data formatting | bytes 4096 | tf_op args[3]
  1.4 67.8 %shard_map.64 = bf16[2048,256]{1,0:T(8,128)(2,1)} custom-call(s32[4]{0:T(128)} %owners.1, s32[128,4]{1,0:T(8,128)} %bitcast.3, f32[64,512]{1,0:T(8,128)} %constant.4.clone.cos_ref, f32[64,512]{1,0:T(8,128)} %constant.5.clone.sin_ref, bf16[4,32,1024]{2,1,0:T(8,128)(2,1)} %spec_ref.1, bf16[4,256,1024]{2,1,0:T(8,128)(2,1)} %pool_hbm.1), custom_call_target="tpu_custom_call" | custom-call | tf_op jit(solution)/shard_map/pallas_call | solution.py:301
  69.3 2.3 %copy.9 = bf16[32,64,256]{2,1,0:T(8,128)(2,1)} copy(bf16[32,64,256]{2,1,0:T(8,128)(2,1)} %bitcast.2) | data formatting | bytes 2097152
